TPU v7x, 256 devices: a whole 4x4x8 slice. The times are simulated.
256 devices in a mesh: tm: 64 (over y_hi, z, x), head: 4 (over y_lo, core).
Axes of the slice: x: 4, y: 4 (y_hi: 2, y_lo: 2; y = y_hi * 2 + y_lo), z: 8, core: 2. Of those that a mesh axis runs over, the one named last changes fastest.
Arguments:
- frames: bfloat16 [64, 512, 1152], P('tm', None, 'head'), may hold values from -6 to 6
- modulation: float32 [3, 1152], replicated, may hold values from -4 to 4
- w_qkv: bfloat16 [3, 1152, 1152], P(None, None, 'head'), may hold values from -1 to 1
- w_out: bfloat16 [1152, 1152], P('head'), may hold values from -0.375 to 0.375
- conv_taps: float32 [3, 1152], P(None, 'head'), may hold values from -3 to 3
- anchors: int32 [4], replicated, may hold values from 0 to 15
Outputs:
- block_out: bfloat16 [64, 512, 1152], P('tm', None, 'head')
All inputs are finite; a program needn't handle non-finite values.
Results may differ from a plain program's by a relative error of at most 0.011.
Values may be sent and summed in bfloat16 or wider, within the bound.
A program may use at most 64 MiB of HBM per device.

v0:
```python
import jax
import jax.numpy as jnp
from jax import lax
from jax.sharding import PartitionSpec as P

HS = 72
SEG = 16


EPSILON = 1e-06


def swapped(block, axis, stride):
    count = lax.axis_size(axis)
    route = []
    for low in range(count):
        high = low | 1 << stride
        if high != low and high < count:
            route += [(low, high), (high, low)]
    return lax.ppermute(block, axis, route)


def extended(x, sides, width):
    for axis, dim in sides:
        size, length = (lax.axis_size(axis), x.shape[dim])
        up = [(i, (i + 1) % size) for i in range(size - 1)]
        down = [(j, i) for i, j in up]
        last = lax.slice_in_dim(x, length - width, length, axis=dim)
        leading = lax.slice_in_dim(x, 0, width, axis=dim)
        before = lax.ppermute(last, axis, up)
        after = lax.ppermute(leading, axis, down)
        x = jnp.concatenate([before, x, after], axis=dim)
    return x


def modulate(frame_rows, modulation):
    values = frame_rows.astype(jnp.float32)
    average = jnp.mean(values, axis=-1, keepdims=True)
    centred = values - average
    variance = jnp.mean(centred * centred, axis=-1, keepdims=True)
    normed = centred * lax.rsqrt(variance + EPSILON)
    return (normed * (1.0 + modulation[1]) + modulation[0]).astype(jnp.bfloat16)


def attend_block(queries, key_rows, value_rows):
    scores = jnp.einsum(
        "qhs,khs->hqk", queries, key_rows, preferred_element_type=jnp.float32
    ) * HS ** (-0.5)
    row_max = jnp.max(scores, axis=-1, keepdims=True)
    weights = jnp.exp(scores - row_max)
    weights = (weights / jnp.sum(weights, axis=-1, keepdims=True)).astype(jnp.bfloat16)
    return jnp.einsum(
        "hqk,khs->qhs", weights, value_rows, preferred_element_type=jnp.float32
    ).astype(jnp.bfloat16)


def local(frames, modulation, w_qkv, w_out, conv_taps, anchors):
    local_frames, tokens, width_dev = frames.shape
    group_size = SEG // local_frames
    tm_pos = lax.axis_index("tm")
    head_pos = lax.axis_index("head")
    gathered = lax.all_gather(frames, "head", axis=2, tiled=True)
    normed = modulate(gathered, modulation)
    projections = jnp.einsum(
        "fpd,cde->cfpe", normed, w_qkv, preferred_element_type=jnp.float32
    ).astype(jnp.bfloat16)
    segment = tm_pos * local_frames // SEG
    anchor_frame = segment * SEG + lax.dynamic_index_in_dim(anchors, segment, 0, keepdims=False)
    is_owner = anchor_frame // local_frames == tm_pos
    anchor_local = anchor_frame % local_frames
    own_part = lax.dynamic_index_in_dim(projections[1:], anchor_local, 1, keepdims=False)
    routed = jnp.where(is_owner, own_part, jnp.zeros_like(own_part))
    for bit_pos in range(group_size.bit_length() - 1):
        routed = routed + swapped(routed, "tm", bit_pos)
    heads_dev = width_dev // HS
    block_rows = min(512, tokens)
    anchor_keys = routed[0].reshape(tokens, heads_dev, HS)
    anchor_values = routed[1].reshape(tokens, heads_dev, HS)

    def frame_attention(pieces):
        queries, own_keys, own_values = pieces
        key_rows = jnp.concatenate([own_keys.reshape(tokens, heads_dev, HS), anchor_keys], axis=0)
        value_rows = jnp.concatenate(
            [own_values.reshape(tokens, heads_dev, HS), anchor_values], axis=0
        )
        query_blocks = queries.reshape(tokens // block_rows, block_rows, heads_dev, HS)

        def one_block(block_queries):
            return attend_block(block_queries, key_rows, value_rows)

        outputs = lax.map(one_block, query_blocks)
        return outputs.reshape(tokens, width_dev)

    attended = lax.map(frame_attention, (projections[0], projections[1], projections[2]))
    partial_terms = jnp.einsum("fpe,ed->fpd", attended, w_out, preferred_element_type=jnp.float32)
    summed = lax.psum_scatter(partial_terms, "head", scatter_dimension=2, tiled=True)
    gate_dev = lax.dynamic_slice_in_dim(modulation[2], head_pos * width_dev, width_dev)
    hidden = (frames.astype(jnp.float32) + gate_dev * summed).astype(jnp.bfloat16)
    padded = extended(hidden, (("tm", 0),), 1).astype(jnp.float32)
    block_out = (
        padded[1:-1]
        + conv_taps[0] * padded[:-2]
        + conv_taps[1] * padded[1:-1]
        + conv_taps[2] * padded[2:]
    )
    return block_out.astype(jnp.bfloat16)


def solution(mesh):
    in_specs = (
        P("tm", None, "head"),
        P(),
        P(None, None, "head"),
        P("head", None),
        P(None, "head"),
        P(),
    )
    out_specs = P("tm", None, "head")
    return jax.shard_map(local, mesh=mesh, in_specs=in_specs, out_specs=out_specs, check_vma=False)
```

profile of v0, /device:TPU:24, one launch (start us, length us, event | category | flops | bytes accessed | tf_op | source)
XLA Modules:
  0.0 227.2 jit_solution(18161637918810966751)
XLA Ops:
  6.5 0.0 copy-start
  6.5 0.0 all-gather.2.cloned.1.call-start
  6.5 0.7 all-gather.2.cloned.1.call-update
  7.3 0.0 all-reduce.3.cloned.1.call-start
  7.3 1.2 dynamic_slice.21
  9.2 0.9 add_reduce_fusion
  10.1 25.4 %all-gather.2.cloned.1.call-done = bf16[1,512,1152]{1,2,0:T(8,128)(2,1)} async-done(((bf16[1,512,288]{1,2,0:T(8,128)(2,1)}), bf16[1,512,1152]{1,2,0:T(8,128)(2,1)}) %all-gather.2.cloned.1.call-update) | async-done | bytes 1179664 | tf_op jit(solution)/shard_map/all_gather | solution.py:62
  35.5 0.0 copy-start.1
  35.5 1.6 convert_reduce_fusion
  37.1 1.6 fusion.8
  38.8 0.0 copy-done
  38.8 0.0 copy-done.1
  38.8 1.4 fusion.12
  40.3 1.5 collective-permute-start
  41.8 13.9 %collective-permute-done = bf16[2,512,288]{1,2,0:T(8,128)(2,1)S(1)} collective-permute-done((bf16[2,512,288]{1,2,0:T(8,128)(2,1)S(1)}, bf16[2,512,288]{1,2,0:T(8,128)(2,1)S(1)}, u32[]{:S(2)}, u32[]{:S(2)}) %collective-permute-start) | collective-permute-done | bytes 589856 | tf_op jit(solution)/shard_map/ppermute | solution.py:20
  55.7 0.1 fusion.47
  55.8 3.1 %collective-permute-start.1 = (bf16[2,512,288]{1,2,0:T(8,128)(2,1)S(1)}, bf16[2,512,288]{1,2,0:T(8,128)(2,1)S(1)}, u32[]{:S(2)}, u32[]{:S(2)}) collective-permute-start(bf16[2,512,288]{1,2,0:T(8,128)(2,1)S(1)} %fusion.47), channel_id=1, source_target_pairs={{0,8},{8,0},{4,12},{12,4},{16,24},{24,16},{20,28},{28,20},{32,40},... | collective-permute-start | bytes 1769480 | tf_op jit(solution)/shard_map/ppermute | solution.py:20
  58.8 13.0 %collective-permute-done.1 = bf16[2,512,288]{1,2,0:T(8,128)(2,1)S(1)} collective-permute-done((bf16[2,512,288]{1,2,0:T(8,128)(2,1)S(1)}, bf16[2,512,288]{1,2,0:T(8,128)(2,1)S(1)}, u32[]{:S(2)}, u32[]{:S(2)}) %collective-permute-start.1) | collective-permute-done | bytes 589856 | tf_op jit(solution)/shard_map/ppermute | solution.py:20
  71.8 0.2 add.93
  72.0 1.6 collective-permute-start.2
  73.6 12.1 %collective-permute-done.2 = bf16[2,512,288]{1,2,0:T(8,128)(2,1)S(1)} collective-permute-done((bf16[2,512,288]{1,2,0:T(8,128)(2,1)S(1)}, bf16[2,512,288]{1,2,0:T(8,128)(2,1)S(1)}, u32[]{:S(2)}, u32[]{:S(2)}) %collective-permute-start.2) | collective-permute-done | bytes 589856 | tf_op jit(solution)/shard_map/ppermute | solution.py:20
  85.7 0.2 add.94
  85.8 2.6 %collective-permute-start.3 = (bf16[2,512,288]{1,2,0:T(8,128)(2,1)S(1)}, bf16[2,512,288]{1,2,0:T(8,128)(2,1)S(1)}, u32[]{:S(2)}, u32[]{:S(2)}) collective-permute-start(bf16[2,512,288]{1,2,0:T(8,128)(2,1)S(1)} %add.94), channel_id=1, source_target_pairs={{0,32},{32,0},{4,36},{36,4},{8,40},{40,8},{12,44},{44,12},{16,48},... | collective-permute-start | bytes 1769480 | tf_op jit(solution)/shard_map/ppermute | solution.py:20
  88.5 0.1 fusion.39
  88.5 23.7 %collective-permute-done.3 = bf16[2,512,288]{1,2,0:T(8,128)(2,1)S(1)} collective-permute-done((bf16[2,512,288]{1,2,0:T(8,128)(2,1)S(1)}, bf16[2,512,288]{1,2,0:T(8,128)(2,1)S(1)}, u32[]{:S(2)}, u32[]{:S(2)}) %collective-permute-start.3) | collective-permute-done | bytes 589856 | tf_op jit(solution)/shard_map/ppermute | solution.py:20
  112.2 0.2 add.95
  112.4 5.0 %fusion.41 = (f32[4,512]{1,0:T(4,128)S(1)}, f32[4,512,1024]{2,1,0:T(8,128)}) fusion(bf16[512,4,72]{0,2,1:T(8,128)(2,1)S(1)} %bitcast.35, bf16[512,4,72]{0,2,1:T(8,128)(2,1)S(1)} %bitcast.37, bf16[512,4,72]{0,2,1:T(8,128)(2,1)S(1)} %bitcast.34), kind=kOutput, calls=%fused_computation.57 | convolution fusion | flops 309462016 | bytes 9281536 | tf_op jit(solution)/shard_map/while/body/eval_jaxpr/while/body/eval_jaxpr/sub | solution.py:50
  117.4 0.0 copy-start.3
  117.4 4.9 %fusion.13 = bf16[4,72,512]{2,1,0:T(8,128)(2,1)S(1)} fusion(f32[4,512,1024]{2,1,0:T(8,128)} %get-tuple-element.58, f32[4,512]{1,0:T(4,128)S(1)} %get-tuple-element.57, bf16[512,4,72]{0,2,1:T(8,128)(2,1)S(1)} %bitcast.36, bf16[512,4,72]{0,2,1:T(8,128)(2,1)S(1)} %bitcast.33), kind=kOutput, calls=%fused_computation.18 | convolution fusion | flops 307511296 | bytes 9281536 | tf_op jit(solution)/shard_map/while/body/eval_jaxpr/while/body/eval_jaxpr/hqk,khs->qhs/dot_general | solution.py:52
  122.3 0.0 copy-done.3
  122.3 2.2 convolution_bitcast_fusion
  124.6 6.4 %copy.23 = f32[1,512,1152]{1,0,2:T(1,128)} copy(f32[1,512,1152]{2,1,0:T(8,128)} %convolution_bitcast_fusion) | data formatting | bytes 4718592 | tf_op jit(solution)/shard_map/fpe,ed->fpd/dot_general | solution.py:95
  131.0 0.0 copy-start.5
  131.0 0.0 copy-start.2
  131.0 0.0 copy-start.4
  131.0 0.0 all-reduce.3.cloned.1.call-update
  131.0 0.6 copy-done.5
  131.6 0.6 dynamic-slice.1
  132.9 0.1 dynamic-slice_reduce_fusion
  133.0 66.6 %all-reduce.3.cloned.1.call-done = f32[1,512,1152]{1,0,2:T(1,128)} async-done(((f32[1,512,1152]{1,0,2:T(1,128)}), f32[1,512,1152]{1,0,2:T(1,128)}) %all-reduce.3.cloned.1.call-update) | async-done | bytes 2359312
  199.6 1.5 constant_dynamic-slice_fusion
  201.1 0.0 copy-done.2
  201.1 0.1 fusion.31
  201.2 3.4 %collective-permute-start.4 = (bf16[1,512,288]{1,2,0:T(8,128)(2,1)S(1)}, bf16[1,512,288]{1,2,0:T(8,128)(2,1)S(1)}, u32[]{:S(2)}, u32[]{:S(2)}) collective-permute-start(bf16[1,512,288]{1,2,0:T(8,128)(2,1)S(1)} %fusion.31), channel_id=1, source_target_pairs={{0,4},{4,8},{8,12},{12,16},{16,20},{20,24},{24,28},{28,32},{32,36}... | collective-permute-start | bytes 884744 | tf_op jit(solution)/shard_map/ppermute | solution.py:30
  204.6 8.2 %collective-permute-start.5 = (bf16[1,512,288]{1,2,0:T(8,128)(2,1)S(1)}, bf16[1,512,288]{1,2,0:T(8,128)(2,1)S(1)}, u32[]{:S(2)}, u32[]{:S(2)}) collective-permute-start(bf16[1,512,288]{1,2,0:T(8,128)(2,1)S(1)} %fusion.31), channel_id=1, source_target_pairs={{4,0},{8,4},{12,8},{16,12},{20,16},{24,20},{28,24},{32,28},{36,32}... | collective-permute-start | bytes 884744 | tf_op jit(solution)/shard_map/ppermute | solution.py:31
  212.8 0.0 copy-done.4
  212.8 5.3 %collective-permute-done.4 = bf16[1,512,288]{1,2,0:T(8,128)(2,1)S(1)} collective-permute-done((bf16[1,512,288]{1,2,0:T(8,128)(2,1)S(1)}, bf16[1,512,288]{1,2,0:T(8,128)(2,1)S(1)}, u32[]{:S(2)}, u32[]{:S(2)}) %collective-permute-start.4) | collective-permute-done | bytes 294944 | tf_op jit(solution)/shard_map/ppermute | solution.py:30
  218.1 1.2 collective-permute-done.5
  219.3 0.1 maximum_convert_fusion
  219.4 0.9 fusion.23
  (5 shorter events, 0.1 us)
Async XLA Ops:
  6.5 32.2 %copy-start = (bf16[3,1152,288]{1,2,0:T(8,128)(2,1)S(1)}, bf16[3,1152,288]{1,2,0:T(8,128)(2,1)}, u32[]{:S(2)}) copy-start(bf16[3,1152,288]{1,2,0:T(8,128)(2,1)} %param.8) | copy-start | bytes 5971972
  6.5 29.0 %all-gather.2.cloned.1.call-start = ((), (), s32[]{:S(2)}) async-start(), calls=%async_computation | async-start | bytes 1474560 | tf_op jit(solution)/shard_map/all_gather | solution.py:62
  7.3 192.3 %all-reduce.3.cloned.1.call-start = ((), (), s32[]{:S(2)}) async-start(), calls=%async_computation.1 | async-start | bytes 4718592
  35.5 3.3 %copy-start.1 = (bf16[1,512,1152]{1,2,0:T(8,128)(2,1)S(1)}, bf16[1,512,1152]{1,2,0:T(8,128)(2,1)}, u32[]{:S(2)}) copy-start(bf16[1,512,1152]{1,2,0:T(8,128)(2,1)} %all-gather.2.cloned.1.call-done) | copy-start | bytes 3538948
  40.3 15.4 %collective-permute-start = (bf16[2,512,288]{1,2,0:T(8,128)(2,1)S(1)}, bf16[2,512,288]{1,2,0:T(8,128)(2,1)S(1)}, u32[]{:S(2)}, u32[]{:S(2)}) collective-permute-start(bf16[2,512,288]{1,2,0:T(8,128)(2,1)S(1)} %fusion.26), channel_id=1, source_target_pairs={{0,4},{4,0},{8,12},{12,8},{16,20},{20,16},{24,28},{28,24},{32,36},... | collective-permute-start | bytes 1769480 | tf_op jit(solution)/shard_map/ppermute | solution.py:20
  55.8 16.1 %collective-permute-start.1 = (bf16[2,512,288]{1,2,0:T(8,128)(2,1)S(1)}, bf16[2,512,288]{1,2,0:T(8,128)(2,1)S(1)}, u32[]{:S(2)}, u32[]{:S(2)}) collective-permute-start(bf16[2,512,288]{1,2,0:T(8,128)(2,1)S(1)} %fusion.47), channel_id=1, source_target_pairs={{0,8},{8,0},{4,12},{12,4},{16,24},{24,16},{20,28},{28,20},{32,40},... | collective-permute-start | bytes 1769480 | tf_op jit(solution)/shard_map/ppermute | solution.py:20
  72.0 13.7 %collective-permute-start.2 = (bf16[2,512,288]{1,2,0:T(8,128)(2,1)S(1)}, bf16[2,512,288]{1,2,0:T(8,128)(2,1)S(1)}, u32[]{:S(2)}, u32[]{:S(2)}) collective-permute-start(bf16[2,512,288]{1,2,0:T(8,128)(2,1)S(1)} %add.93), channel_id=1, source_target_pairs={{0,16},{16,0},{4,20},{20,4},{8,24},{24,8},{12,28},{28,12},{32,48},... | collective-permute-start | bytes 1769480 | tf_op jit(solution)/shard_map/ppermute | solution.py:20
  85.8 26.4 %collective-permute-start.3 = (bf16[2,512,288]{1,2,0:T(8,128)(2,1)S(1)}, bf16[2,512,288]{1,2,0:T(8,128)(2,1)S(1)}, u32[]{:S(2)}, u32[]{:S(2)}) collective-permute-start(bf16[2,512,288]{1,2,0:T(8,128)(2,1)S(1)} %add.94), channel_id=1, source_target_pairs={{0,32},{32,0},{4,36},{36,4},{8,40},{40,8},{12,44},{44,12},{16,48},... | collective-permute-start | bytes 1769480 | tf_op jit(solution)/shard_map/ppermute | solution.py:20
  117.4 4.9 %copy-start.3 = (bf16[288,1152]{1,0:T(8,128)(2,1)S(1)}, bf16[288,1152]{1,0:T(8,128)(2,1)}, u32[]{:S(2)}) copy-start(bf16[288,1152]{1,0:T(8,128)(2,1)} %param.9) | copy-start | bytes 1990660
  131.0 0.7 copy-start.5
  131.0 70.1 %copy-start.2 = (bf16[1,512,288]{1,2,0:T(8,128)(2,1)S(1)}, bf16[1,512,288]{1,2,0:T(8,128)(2,1)}, u32[]{:S(2)}) copy-start(bf16[1,512,288]{1,2,0:T(8,128)(2,1)} %param.6) | copy-start | bytes 884740
  131.0 81.8 %copy-start.4 = (f32[3,288]{1,0:T(4,128)S(1)}, f32[3,288]{1,0:T(4,128)}, u32[]{:S(2)}) copy-start(f32[3,288]{1,0:T(4,128)} %param.10) | copy-start | bytes 10372
  201.2 16.9 %collective-permute-start.4 = (bf16[1,512,288]{1,2,0:T(8,128)(2,1)S(1)}, bf16[1,512,288]{1,2,0:T(8,128)(2,1)S(1)}, u32[]{:S(2)}, u32[]{:S(2)}) collective-permute-start(bf16[1,512,288]{1,2,0:T(8,128)(2,1)S(1)} %fusion.31), channel_id=1, source_target_pairs={{0,4},{4,8},{8,12},{12,16},{16,20},{20,24},{24,28},{28,32},{32,36}... | collective-permute-start | bytes 884744 | tf_op jit(solution)/shard_map/ppermute | solution.py:30
  204.6 14.7 %collective-permute-start.5 = (bf16[1,512,288]{1,2,0:T(8,128)(2,1)S(1)}, bf16[1,512,288]{1,2,0:T(8,128)(2,1)S(1)}, u32[]{:S(2)}, u32[]{:S(2)}) collective-permute-start(bf16[1,512,288]{1,2,0:T(8,128)(2,1)S(1)} %fusion.31), channel_id=1, source_target_pairs={{4,0},{8,4},{12,8},{16,12},{20,16},{24,20},{28,24},{32,28},{36,32}... | collective-permute-start | bytes 884744 | tf_op jit(solution)/shard_map/ppermute | solution.py:31
Sparse Core Ops, SparseCore 0:
  9.1 26.3 all-gather.1
  131.1 68.4 all-reduce.2
where the time goes:
time: 228 us; the launch traced here: 227 us
  waiting for transfers between devices  162 us (71%)
  starting transfers between devices  20.5 us (9%)
  between operations  14.9 us (7%)
  matrix products  13.5 us (6%)
  local copies, waits for them, and re-layouts  10.6 us (5%)
  other arithmetic  5.89 us (3%)
    unnamed x3, waiting for transfers between devices  67.3 us
    ppermute x4, waiting for transfers between devices, swapped(): return lax.ppermute(block, axis, route)  62.6 us
    all_gather x1, waiting for transfers between devices, local(): gathered = lax.all_gather(frames, 'head', axis=2, tiled=True)  25.4 us
    ppermute x4, starting transfers between devices, swapped(): return lax.ppermute(block, axis, route)  8.88 us
    ppermute x1, starting transfers between devices, extended(): after = lax.ppermute(leading, axis, down)  8.19 us
    dot_general x1, local copies, waits for them, and re-layouts, local(): jnp.einsum('fpe,ed->fpd', attended, w_out, preferred_element_type=jnp.flo...  6.39 us
    ppermute x1, waiting for transfers between devices, extended(): before = lax.ppermute(last, axis, up)  5.26 us
    sub x1, matrix products, attend_block(): weights = jnp.exp(scores - row_max)  4.96 us
  transfers between devices with their start and end apart: 8, of which 8 were waited for; matrix products, arithmetic and copies ran while one was open for 1% of the time, Pallas kernels for 0%

commit v1 on v0

v1 whole, which is shorter than its diff:
```python
import jax
import jax.numpy as jnp
from jax import lax
from jax.experimental import pallas as pl
from jax.experimental.pallas import tpu as pltpu
from jax.sharding import PartitionSpec as P

HS = 72
SEG = 16
LINE = 4
EPSILON = 1e-06
PAD = 128
VROWS = 80
ROWS, COLS = 96, 128
LAG = 2
HALF = 256
MESH = pl.DeviceIdType.MESH
F32, BF16 = jnp.float32, jnp.bfloat16


def dot(a, b):
    return jnp.dot(a, b, preferred_element_type=F32)


def kernel(
    x_ref, mod_ref, wqkv_ref, wo_ref, taps_ref, anchors_ref, out_ref,
    xf, xa, zup, zdn, szup, szdn, base, xr, xl, sxr, sxl,
    modt, tapst, wot, qs, ks, vs, os_, ms, at,
    ps, pr, keep, ys, yr, hs, hl, hr,
    own_send, own_y, own_c, own_f,
    flow_send, up_recv, dn_recv, xr_recv, xl_recv,
    anc_send, anc_y, anc_c, anc_f,
    rs_send, rs_c, rs_y, halo_send, halo_l, halo_r,
):
    width, tokens = x_ref.shape
    heads = width // HS
    per_col = width // ROWS
    pieces = per_col * (tokens // COLS)
    halves = tokens // HALF
    d = xf.shape[0]
    tm, head = lax.axis_index("tm"), lax.axis_index("head")
    frames = lax.axis_size("tm")
    xpos = lax.rem(tm, LINE)
    zpos = lax.rem(tm // LINE, LINE)
    sib = head + 1 - 2 * lax.rem(head, 2)
    far = lax.rem(head + 2, 4)
    far_sib = lax.rem(sib + 2, 4)
    anchor = anchors_ref[tm // SEG]
    ax, az = lax.rem(anchor, LINE), anchor // LINE
    is_src = jnp.logical_and(ax == xpos, az == zpos)

    def remote(src, dst, send, recv, to_tm, to_head):
        return pltpu.make_async_remote_copy(
            src_ref=src, dst_ref=dst, send_sem=send, recv_sem=recv,
            device_id=(to_tm, to_head), device_id_type=MESH)

    barrier = pltpu.get_barrier_semaphore()

    def greet(to_tm, to_head):
        pl.semaphore_signal(barrier, inc=1, device_id=(to_tm, to_head), device_id_type=MESH)

    greet(tm, sib)
    greet(tm, far)
    links = ((tm > 0, tm - 1), (tm < frames - 1, tm + 1),
             (zpos > 0, tm - LINE), (zpos < LINE - 1, tm + LINE))
    count = jnp.int32(2)
    for there, who in links:
        @pl.when(there)
        def _(who=who):
            greet(who, head)
        count = count + there.astype(jnp.int32)
    pl.semaphore_wait(barrier, count)

    def rows_of(ref, j, cols):
        return ref.at[pl.ds(pl.multiple_of(j * width, 32), width), cols]

    def half(t):
        return pl.ds(t * HALF, HALF)

    def own_copy(t, to, send, recv):
        return remote(x_ref.at[:, half(t)], rows_of(xf, head, half(t)), send, recv, tm, to)

    def own_forward(t):
        return remote(rows_of(xf, far, half(t)), rows_of(xf, far, half(t)),
                      own_send.at[2, t], own_f.at[t], tm, sib)

    def own_start():
        for t in range(halves):
            own_copy(t, far, own_send.at[0, t], own_y.at[t]).start()
            own_copy(t, sib, own_send.at[1, t], own_c.at[t]).start()
        xf[pl.ds(pl.multiple_of(head * width, 32), width), :] = x_ref[...]

    def own_pass(t):
        own_copy(t, far, own_send.at[0, t], own_y.at[t]).wait_recv()
        own_forward(t).start()

    def piece(ref, p, off=0):
        f, c = lax.rem(p, per_col), p // per_col
        row = off + f * ROWS
        if not isinstance(row, int):
            row = pl.multiple_of(row, 32)
        col = c * COLS
        if not isinstance(col, int):
            col = pl.multiple_of(col, 128)
        return ref.at[pl.ds(row, ROWS), pl.ds(col, COLS)]

    def flow(s, place, stride, n, origin, src_here, got, sent, recv):
        p = s - LAG * place
        live = jnp.logical_and(p >= 0, p < pieces)
        nxt = tm + stride

        @pl.when(jnp.logical_and(live, place == 0))
        def _():
            remote(piece(origin, p), piece(got, p), flow_send.at[n], recv.at[p], nxt, head).start()

        @pl.when(jnp.logical_and(live, place > 0))
        def _():
            remote(piece(sent, p), piece(got, p), flow_send.at[n], recv.at[p], nxt, head).wait_recv()

            @pl.when(place < LINE - 1)
            def _():
                piece(sent, p)[...] = jnp.where(src_here, piece(origin, p)[...], piece(got, p)[...])
                remote(piece(sent, p), piece(got, p), flow_send.at[n], recv.at[p], nxt, head).start()

    def flow_end(place, stride, n, sent, recv):
        @pl.when(place < LINE - 1)
        def _():
            remote(sent, sent, flow_send.at[n], recv.at[0], tm + stride, head).wait_send()

    mine = head * width

    def anc_copy(p, to, send, recv):
        return remote(piece(xa, p, mine), piece(xa, p, mine), send, recv.at[p], tm, to)

    def anc_forward(p):
        return remote(piece(xa, p, far * width), piece(xa, p, far * width),
                      anc_send.at[2], anc_f.at[p], tm, sib)

    steps = pieces + 7 * LAG

    def step(s):
        flow(s, zpos, LINE, 0, x_ref, is_src, zup, szup, up_recv)
        flow(s, LINE - 1 - zpos, -LINE, 1, x_ref, is_src, zdn, szdn, dn_recv)
        p = s - 3 * LAG
        if 0 <= p < pieces:
            piece(base, p)[...] = jnp.where(
                is_src, piece(x_ref, p)[...],
                jnp.where(az < zpos, piece(zup, p)[...], piece(zdn, p)[...]))
        flow(p, xpos, 1, 2, base, ax == xpos, xr, sxr, xr_recv)
        flow(p, LINE - 1 - xpos, -1, 3, base, ax == xpos, xl, sxl, xl_recv)
        p = s - 6 * LAG
        if 0 <= p < pieces:
            piece(xa, p, mine)[...] = jnp.where(
                ax == xpos, piece(base, p)[...],
                jnp.where(ax < xpos, piece(xr, p)[...], piece(xl, p)[...]))
            anc_copy(p, far, anc_send.at[0], anc_y).start()
            anc_copy(p, sib, anc_send.at[1], anc_c).start()
        p = s - 7 * LAG
        if 0 <= p < pieces:
            anc_copy(p, far, anc_send.at[0], anc_y).wait_recv()
            anc_forward(p).start()

    def norm_project(src, t, first):
        v = src[:, half(t)].astype(F32)
        v = v - jnp.mean(v, axis=0, keepdims=True)
        r = lax.rsqrt(jnp.mean(v * v, axis=0, keepdims=True) + EPSILON)
        n = (v * r * (1.0 + modt[:, 1:2]) + modt[:, 0:1]).astype(BF16)
        return dot(wqkv_ref[first:, :], n)

    def put_kv(kv, t, offset):
        spot = pl.ds(offset + t * HALF, HALF)
        zeros = jnp.zeros((PAD - HS, HALF), F32)
        ones = jnp.where(lax.broadcasted_iota(jnp.int32, (VROWS - HS, HALF), 0) == 0, 1.0, 0.0)
        for h in range(heads):
            k = kv[h * HS:(h + 1) * HS]
            ks[h, spot, :] = jnp.concatenate([k, zeros], axis=0).T.astype(BF16)
            v = kv[width + h * HS:width + (h + 1) * HS]
            vs[h, :, spot] = jnp.concatenate([v, ones], axis=0).astype(BF16)

    def own_qkv(t):
        for wait in (own_copy(t, sib, own_send.at[1, t], own_c.at[t]), own_forward(t)):
            wait.wait_recv()
        qkv = norm_project(xf, t, 0)
        zeros = jnp.zeros((PAD - HS, HALF), F32)
        for h in range(heads):
            q = qkv[h * HS:(h + 1) * HS]
            qs[h, :, half(t)] = jnp.concatenate([q, zeros], axis=0).astype(BF16)
        put_kv(qkv[width:], t, 0)

    exponent = HS ** (-0.5) * 1.4426950408889634

    def attend_own(h, t):
        s = dot(ks[h, :tokens, :], qs[h, :, half(t)])
        m = jnp.max(s, axis=0, keepdims=True)
        p = jnp.exp2((s - m) * exponent).astype(BF16)
        os_[h, :, half(t)] = dot(vs[h, :, :tokens], p)
        ms[h, :, half(t)] = m

    def attend_anchor(h, t):
        s = dot(ks[h, tokens:, :], qs[h, :, half(t)])
        m0 = ms[h, :, half(t)]
        m = jnp.maximum(m0, jnp.max(s, axis=0, keepdims=True))
        p = jnp.exp2((s - m) * exponent).astype(BF16)
        o = os_[h, :, half(t)] * jnp.exp2((m0 - m) * exponent) + dot(vs[h, :, tokens:], p)
        at[h * HS:(h + 1) * HS, half(t)] = o[:HS] / o[HS:HS + 1]

    def rs_core(t, i):
        return remote(ps.at[i, :, half(t)], pr.at[i, :, half(t)],
                      rs_send.at[i, t], rs_c.at[i, t], tm, sib)

    def rs_far(t):
        return remote(ys.at[:, half(t)], yr.at[:, half(t)], rs_send.at[2, t], rs_y.at[t], tm, far)

    def project(t):
        a = at[:, half(t)].astype(BF16)

        def block(j):
            return dot(wot[pl.ds(pl.multiple_of(j * width, 32), width), :], a)

        for i, j in enumerate((far_sib, sib)):
            ps[1 - i, :, half(t)] = block(j).astype(BF16)
            rs_core(t, 1 - i).start()
        keep[1, :, half(t)] = block(far)
        keep[0, :, half(t)] = block(head)

    def sum_core(t):
        rs_core(t, 1).wait_recv()
        ys[:, half(t)] = (keep[1, :, half(t)] + pr[1, :, half(t)].astype(F32)).astype(BF16)
        rs_far(t).start()

    def halo_next(t):
        return remote(hs.at[:, half(t)], hl.at[:, half(t)], halo_send.at[0, t], halo_l.at[t], tm + 1, head)

    def halo_prev(t):
        return remote(hs.at[:, half(t)], hr.at[:, half(t)], halo_send.at[1, t], halo_r.at[t], tm - 1, head)

    has_next, has_prev = tm < frames - 1, tm > 0

    def sum_far(t):
        rs_core(t, 0).wait_recv()
        own = keep[0, :, half(t)] + pr[0, :, half(t)].astype(F32)
        rs_far(t).wait_recv()
        gate = modt[pl.ds(pl.multiple_of(head * width, 32), width), 2:3]
        total = own + yr[:, half(t)].astype(F32)
        hs[:, half(t)] = (x_ref[:, half(t)].astype(F32) + gate * total).astype(BF16)

        @pl.when(has_next)
        def _():
            halo_next(t).start()

        @pl.when(has_prev)
        def _():
            halo_prev(t).start()

    def finish(t):
        @pl.when(has_prev)
        def _():
            halo_next(t).wait_recv()

        @pl.when(has_next)
        def _():
            halo_prev(t).wait_recv()

        h = hs[:, half(t)].astype(F32)
        out_ref[:, half(t)] = (
            h + tapst[:, 0:1] * hl[:, half(t)].astype(F32)
            + tapst[:, 1:2] * h + tapst[:, 2:3] * hr[:, half(t)].astype(F32)
        ).astype(BF16)

    own_start()
    work = {}

    def after(s, fn, *args):
        work.setdefault(s, []).append((fn, args))

    def setup():
        modt[...] = mod_ref[...].T
        tapst[...] = taps_ref[...].T
        wot[...] = wo_ref[...].T

        @pl.when(jnp.logical_not(has_prev))
        def _():
            hl[...] = jnp.zeros_like(hl)

        @pl.when(jnp.logical_not(has_next))
        def _():
            hr[...] = jnp.zeros_like(hr)

    after(1, setup)
    after(6, own_pass, 0)
    after(9, own_qkv, 0)
    after(11, own_pass, 1)
    after(13, own_qkv, 1)
    units = [(h, t) for t in range(halves) for h in range(heads)]
    for i, (h, t) in enumerate(units):
        after(14 + i, attend_own, h, t)
    for s in range(steps):
        step(s)
        for fn, args in work.get(s, ()):
            fn(*args)

    def anchor_kv(t):
        for p in range(t * HALF // COLS * per_col, (t + 1) * HALF // COLS * per_col):
            anc_copy(p, sib, anc_send.at[1], anc_c).wait_recv()
            anc_forward(p).wait_recv()
        put_kv(norm_project(xa, t, width), t, tokens)

    for t in range(halves):
        anchor_kv(t)
    for h in range(heads):
        attend_anchor(h, 0)
    project(0)
    attend_anchor(0, 1)
    sum_core(0)
    for h in range(1, heads):
        attend_anchor(h, 1)
    project(1)
    sum_far(0)
    sum_core(1)
    finish(0)
    sum_far(1)
    finish(1)

    flow_end(zpos, LINE, 0, szup, up_recv)
    flow_end(LINE - 1 - zpos, -LINE, 1, szdn, dn_recv)
    flow_end(xpos, 1, 2, sxr, xr_recv)
    flow_end(LINE - 1 - xpos, -1, 3, sxl, xl_recv)
    shard = rows_of(xa, head, pl.ds(0, tokens))
    for n, to in ((0, far), (1, sib), (2, sib)):
        remote(shard, shard, anc_send.at[n], anc_y.at[0], tm, to).wait_send()
    for t in range(halves):
        own_copy(t, far, own_send.at[0, t], own_y.at[t]).wait_send()
        own_copy(t, sib, own_send.at[1, t], own_c.at[t]).wait_send()
        own_forward(t).wait_send()
        rs_core(t, 0).wait_send()
        rs_core(t, 1).wait_send()
        rs_far(t).wait_send()

        @pl.when(has_next)
        def _():
            halo_next(t).wait_send()

        @pl.when(has_prev)
        def _():
            halo_prev(t).wait_send()


def local(frames, modulation, w_qkv, w_out, conv_taps, anchors):
    _, tokens, width = frames.shape
    d = w_qkv.shape[1]
    heads = width // HS
    halves = tokens // HALF
    pieces = (width // ROWS) * (tokens // COLS)
    x_t = jnp.swapaxes(frames[0], 0, 1)
    w_t = jnp.swapaxes(w_qkv, 1, 2).reshape(3 * width, d)
    shard = pltpu.VMEM((width, tokens), BF16)
    dma = pltpu.SemaphoreType.DMA
    vmem = pl.BlockSpec(memory_space=pltpu.VMEM)
    out = pl.pallas_call(
        kernel,
        out_shape=jax.ShapeDtypeStruct((width, tokens), BF16),
        in_specs=[vmem] * 5 + [pl.BlockSpec(memory_space=pltpu.SMEM)],
        out_specs=vmem,
        scratch_shapes=[
            pltpu.VMEM((d, tokens), BF16), pltpu.VMEM((d, tokens), BF16),
            *[shard] * 9,
            pltpu.VMEM((d, 3), F32), pltpu.VMEM((width, 3), F32), pltpu.VMEM((d, width), BF16),
            pltpu.VMEM((heads, PAD, tokens), BF16),
            pltpu.VMEM((heads, 2 * tokens, PAD), BF16),
            pltpu.VMEM((heads, VROWS, 2 * tokens), BF16),
            pltpu.VMEM((heads, VROWS, tokens), F32),
            pltpu.VMEM((heads, 1, tokens), F32),
            pltpu.VMEM((width, tokens), F32),
            pltpu.VMEM((2, width, tokens), BF16), pltpu.VMEM((2, width, tokens), BF16),
            pltpu.VMEM((2, width, tokens), F32),
            *[shard] * 5,
            dma((3, halves)), dma((halves,)), dma((halves,)), dma((halves,)),
            dma((4,)), dma((pieces,)), dma((pieces,)), dma((pieces,)), dma((pieces,)),
            dma((3,)), dma((pieces,)), dma((pieces,)), dma((pieces,)),
            dma((3, halves)), dma((2, halves)), dma((halves,)),
            dma((2, halves)), dma((halves,)), dma((halves,)),
        ],
        compiler_params=pltpu.CompilerParams(
            collective_id=0, has_side_effects=True, vmem_limit_bytes=60 * 1024 * 1024),
        name="block",
    )(x_t, modulation, w_t, w_out, conv_taps, anchors)
    return jnp.swapaxes(out, 0, 1)[None]


def solution(mesh):
    in_specs = (
        P("tm", None, "head"),
        P(),
        P(None, None, "head"),
        P("head", None),
        P(None, "head"),
        P(),
    )
    out_specs = P("tm", None, "head")
    return jax.shard_map(local, mesh=mesh, in_specs=in_specs, out_specs=out_specs, check_vma=False)
```

time: 228 us -> 76.1 us (0.33)
  waiting for transfers between devices: 162 us -> 0 us
  Pallas kernels: 0 us -> 73.4 us
  starting transfers between devices: 20.5 us -> 0 us
  between operations: 14.9 us -> 0.01 us
  matrix products: 13.5 us -> 0 us
  local copies, waits for them, and re-layouts: 10.6 us -> 1.69 us
  other arithmetic: 5.89 us -> 0 us
    pallas_call x0 -> x1, Pallas kernels: none -> 73.4 us  [local(): pl.pallas_call(kernel, out_shape=jax.ShapeDtypeStruct((width, tokens), BF...]
    ppermute x6 -> x0, waiting for transfers between devices: 69.1 us -> none  [the longest x4 62.6 us: swapped(): return lax.ppermute(block, axis, route)]
    unnamed x3 -> x0, waiting for transfers between devices: 67.3 us -> none
    all_gather x1 -> x0, waiting for transfers between devices: 25.4 us -> none  [local(): gathered = lax.all_gather(frames, 'head', axis=2, tiled=True)]
    ppermute x6 -> x0, starting transfers between devices: 20.4 us -> none  [the longest x4 8.88 us: swapped(): return lax.ppermute(block, axis, route)]
    dot_general x3 -> x0, matrix products: 8.58 us -> none  [the longest x1 4.91 us: attend_block(): jnp.einsum('hqk,khs->qhs', weights, value_rows, preferred_element_type=jn...]
    dot_general x1 -> x0, local copies, waits for them, and re-layouts: 6.39 us -> none  [local(): jnp.einsum('fpe,ed->fpd', attended, w_out, preferred_element_type=jnp.flo...]
    sub x1 -> x0, matrix products: 4.96 us -> none  [attend_block(): weights = jnp.exp(scores - row_max)]
  transfers between devices with their start and end apart: 8 -> 0, of which waited for: 8 -> 0; matrix products, arithmetic and copies ran while one was open for 1% -> 0% of each run, Pallas kernels for 0% -> 0%
where the time goes in v1:
time: 76.1 us; the launch traced here: 75.1 us
  Pallas kernels  73.4 us (96%)
  local copies, waits for them, and re-layouts  1.69 us (2%)
    pallas_call x1, Pallas kernels, local(): pl.pallas_call(kernel, out_shape=jax.ShapeDtypeStruct((width, tokens), BF...  73.4 us
    unnamed x1, local copies, waits for them, and re-layouts  1.69 us

profile of v1, /device:TPU:24, one launch (start us, length us, event | category | flops | bytes accessed | tf_op | source)
XLA Modules:
  0.0 75.1 jit_solution(11490282117825244283)
XLA Ops:
  0.0 73.4 %block.1 = bf16[288,512]{1,0:T(8,128)(2,1)} custom-call(bf16[288,512]{1,0:T(8,128)(2,1)} %bitcast.11, f32[3,1152]{1,0:T(4,128)} %mod_ref.1, bf16[864,1152]{1,0:T(8,128)(2,1)} %bitcast.9, bf16[288,1152]{1,0:T(8,128)(2,1)} %wo_ref.1, f32[3,288]{1,0:T(4,128)} %taps_ref.1, s32[4]{0:T(128)} %anchors_ref.1), custom_call_target="tpu_custom_call" | custom-call | tf_op jit(solution)/shard_map/block/pallas_call | solution.py:359
  73.4 1.7 %copy.8 = bf16[1,512,288]{1,2,0:T(8,128)(2,1)} copy(bf16[1,512,288]{1,2,0:T(8,128)(2,1)} %bitcast.10) | data formatting | bytes 589824

commit v2 on v1

--- a/solution.py
+++ b/solution.py
@@ -11,7 +11,7 @@
 EPSILON = 1e-06
 PAD = 128
 VROWS = 80
-ROWS, COLS = 96, 128
+ROWS, COLS = 96, 256
 LAG = 2
 HALF = 256
 MESH = pl.DeviceIdType.MESH
@@ -189,20 +189,22 @@
 
     exponent = HS ** (-0.5) * 1.4426950408889634
 
-    def attend_own(h, t):
-        s = dot(ks[h, :tokens, :], qs[h, :, half(t)])
+    def attend(h, t, lo, size, first, last):
+        keys = pl.ds(lo, size)
+        s = dot(ks[h, keys, :], qs[h, :, half(t)])
         m = jnp.max(s, axis=0, keepdims=True)
+        if not first:
+            before = ms[h, :, half(t)]
+            m = jnp.maximum(before, m)
         p = jnp.exp2((s - m) * exponent).astype(BF16)
-        os_[h, :, half(t)] = dot(vs[h, :, :tokens], p)
-        ms[h, :, half(t)] = m
-
-    def attend_anchor(h, t):
-        s = dot(ks[h, tokens:, :], qs[h, :, half(t)])
-        m0 = ms[h, :, half(t)]
-        m = jnp.maximum(m0, jnp.max(s, axis=0, keepdims=True))
-        p = jnp.exp2((s - m) * exponent).astype(BF16)
-        o = os_[h, :, half(t)] * jnp.exp2((m0 - m) * exponent) + dot(vs[h, :, tokens:], p)
-        at[h * HS:(h + 1) * HS, half(t)] = o[:HS] / o[HS:HS + 1]
+        o = dot(vs[h, :, keys], p)
+        if not first:
+            o = os_[h, :, half(t)] * jnp.exp2((before - m) * exponent) + o
+        if last:
+            at[h * HS:(h + 1) * HS, half(t)] = o[:HS] / o[HS:HS + 1]
+        else:
+            os_[h, :, half(t)] = o
+            ms[h, :, half(t)] = m
 
     def rs_core(t, i):
         return remote(ps.at[i, :, half(t)], pr.at[i, :, half(t)],
@@ -286,40 +288,45 @@
         def _():
             hr[...] = jnp.zeros_like(hr)
 
-    after(1, setup)
-    after(6, own_pass, 0)
-    after(9, own_qkv, 0)
-    after(11, own_pass, 1)
-    after(13, own_qkv, 1)
-    units = [(h, t) for t in range(halves) for h in range(heads)]
-    for i, (h, t) in enumerate(units):
-        after(14 + i, attend_own, h, t)
-    for s in range(steps):
-        step(s)
-        for fn, args in work.get(s, ()):
-            fn(*args)
-
     def anchor_kv(t):
         for p in range(t * HALF // COLS * per_col, (t + 1) * HALF // COLS * per_col):
             anc_copy(p, sib, anc_send.at[1], anc_c).wait_recv()
             anc_forward(p).wait_recv()
         put_kv(norm_project(xa, t, width), t, tokens)
 
+    units = [(h, t) for t in range(halves) for h in range(heads)]
+    after(1, setup)
+    after(3, own_pass, 0)
+    after(5, own_pass, 1)
+    after(5, own_qkv, 0)
+    after(7, own_qkv, 1)
+    for i, (h, t) in enumerate(units):
+        after(8 + i, attend, h, t, 0, tokens, True, False)
+    after(18, anchor_kv, 0)
+    for i, (h, t) in enumerate(units):
+        after(18 + i // 4, attend, h, t, tokens, HALF, False, False)
+    for s in range(steps):
+        step(s)
+        for fn, args in work.get(s, ()):
+            fn(*args)
+
+    def last(h, t):
+        attend(h, t, tokens + HALF, HALF, False, True)
+
+    anchor_kv(1)
+    for h in range(heads):
+        last(h, 0)
+    project(0)
+    for h in range(heads - 1):
+        last(h, 1)
+    sum_core(0)
+    last(heads - 1, 1)
+    project(1)
+    sum_core(1)
     for t in range(halves):
-        anchor_kv(t)
-    for h in range(heads):
-        attend_anchor(h, 0)
-    project(0)
-    attend_anchor(0, 1)
-    sum_core(0)
-    for h in range(1, heads):
-        attend_anchor(h, 1)
-    project(1)
-    sum_far(0)
-    sum_core(1)
-    finish(0)
-    sum_far(1)
-    finish(1)
+        sum_far(t)
+    for t in range(halves):
+        finish(t)
 
     flow_end(zpos, LINE, 0, szup, up_recv)
     flow_end(LINE - 1 - zpos, -LINE, 1, szdn, dn_recv)

time: 76.1 us -> 64.1 us (0.84); the launches traced: 75.1 us -> 64 us
  Pallas kernels: 73.4 us -> 62.3 us
    pallas_call x1, Pallas kernels: 73.4 us -> 62.3 us  [local(): pl.pallas_call(kernel, out_shape=jax.ShapeDtypeStruct((width, tokens), BF...]
where the time goes in v2:
time: 64.1 us; the launch traced here: 64 us
  Pallas kernels  62.3 us (97%)
  local copies, waits for them, and re-layouts  1.69 us (3%)
    pallas_call x1, Pallas kernels, local(): pl.pallas_call(kernel, out_shape=jax.ShapeDtypeStruct((width, tokens), BF...  62.3 us
    unnamed x1, local copies, waits for them, and re-layouts  1.69 us

profile of v2, /device:TPU:24, one launch (start us, length us, event | category | flops | bytes accessed | tf_op | source)
XLA Modules:
  0.0 64.0 jit_solution(2041632292846239029)
XLA Ops:
  0.0 62.3 %block.1 = bf16[288,512]{1,0:T(8,128)(2,1)} custom-call(bf16[288,512]{1,0:T(8,128)(2,1)} %bitcast.11, f32[3,1152]{1,0:T(4,128)} %mod_ref.1, bf16[864,1152]{1,0:T(8,128)(2,1)} %bitcast.9, bf16[288,1152]{1,0:T(8,128)(2,1)} %wo_ref.1, f32[3,288]{1,0:T(4,128)} %taps_ref.1, s32[4]{0:T(128)} %anchors_ref.1), custom_call_target="tpu_custom_call" | custom-call | tf_op jit(solution)/shard_map/block/pallas_call | solution.py:366
  62.3 1.7 %copy.8 = bf16[1,512,288]{1,2,0:T(8,128)(2,1)} copy(bf16[1,512,288]{1,2,0:T(8,128)(2,1)} %bitcast.10) | data formatting | bytes 589824

commit v3 on v2

--- a/solution.py
+++ b/solution.py
@@ -11,8 +11,8 @@
 EPSILON = 1e-06
 PAD = 128
 VROWS = 80
-ROWS, COLS = 96, 256
-LAG = 2
+COLS = 128
+PARTS = 2
 HALF = 256
 MESH = pl.DeviceIdType.MESH
 F32, BF16 = jnp.float32, jnp.bfloat16
@@ -24,18 +24,17 @@
 
 def kernel(
     x_ref, mod_ref, wqkv_ref, wo_ref, taps_ref, anchors_ref, out_ref,
-    xf, xa, zup, zdn, szup, szdn, base, xr, xl, sxr, sxl,
+    xf, xa, got_x, here_x, got_z,
     modt, tapst, wot, qs, ks, vs, os_, ms, at,
     ps, pr, keep, ys, yr, hs, hl, hr,
     own_send, own_y, own_c, own_f,
-    flow_send, up_recv, dn_recv, xr_recv, xl_recv,
+    row_send, row_recv, col_send, col_recv, all_send, all_recv,
     anc_send, anc_y, anc_c, anc_f,
     rs_send, rs_c, rs_y, halo_send, halo_l, halo_r,
 ):
     width, tokens = x_ref.shape
     heads = width // HS
-    per_col = width // ROWS
-    pieces = per_col * (tokens // COLS)
+    rows = width // PARTS
     halves = tokens // HALF
     d = xf.shape[0]
     tm, head = lax.axis_index("tm"), lax.axis_index("head")
@@ -47,7 +46,7 @@
     far_sib = lax.rem(sib + 2, 4)
     anchor = anchors_ref[tm // SEG]
     ax, az = lax.rem(anchor, LINE), anchor // LINE
-    is_src = jnp.logical_and(ax == xpos, az == zpos)
+    from_x, from_z = lax.rem(xpos - ax + LINE, LINE), lax.rem(zpos - az + LINE, LINE)
 
     def remote(src, dst, send, recv, to_tm, to_head):
         return pltpu.make_async_remote_copy(
@@ -61,10 +60,17 @@
 
     greet(tm, sib)
     greet(tm, far)
-    links = ((tm > 0, tm - 1), (tm < frames - 1, tm + 1),
-             (zpos > 0, tm - LINE), (zpos < LINE - 1, tm + LINE))
-    count = jnp.int32(2)
-    for there, who in links:
+    def in_row(k):
+        return tm - xpos + lax.rem(xpos + k, LINE)
+
+    def in_column(k):
+        return tm + LINE * (lax.rem(zpos + k, LINE) - zpos)
+
+    for k in range(1, LINE):
+        greet(in_row(k), head)
+        greet(in_column(k), head)
+    count = jnp.int32(2 * LINE)
+    for there, who in ((tm > 0, tm - 1), (tm < frames - 1, tm + 1)):
         @pl.when(there)
         def _(who=who):
             greet(who, head)
@@ -94,74 +100,74 @@
         own_copy(t, far, own_send.at[0, t], own_y.at[t]).wait_recv()
         own_forward(t).start()
 
-    def piece(ref, p, off=0):
-        f, c = lax.rem(p, per_col), p // per_col
-        row = off + f * ROWS
-        if not isinstance(row, int):
-            row = pl.multiple_of(row, 32)
-        col = c * COLS
-        if not isinstance(col, int):
-            col = pl.multiple_of(col, 128)
-        return ref.at[pl.ds(row, ROWS), pl.ds(col, COLS)]
-
-    def flow(s, place, stride, n, origin, src_here, got, sent, recv):
-        p = s - LAG * place
-        live = jnp.logical_and(p >= 0, p < pieces)
-        nxt = tm + stride
-
-        @pl.when(jnp.logical_and(live, place == 0))
-        def _():
-            remote(piece(origin, p), piece(got, p), flow_send.at[n], recv.at[p], nxt, head).start()
-
-        @pl.when(jnp.logical_and(live, place > 0))
-        def _():
-            remote(piece(sent, p), piece(got, p), flow_send.at[n], recv.at[p], nxt, head).wait_recv()
-
-            @pl.when(place < LINE - 1)
-            def _():
-                piece(sent, p)[...] = jnp.where(src_here, piece(origin, p)[...], piece(got, p)[...])
-                remote(piece(sent, p), piece(got, p), flow_send.at[n], recv.at[p], nxt, head).start()
-
-    def flow_end(place, stride, n, sent, recv):
-        @pl.when(place < LINE - 1)
-        def _():
-            remote(sent, sent, flow_send.at[n], recv.at[0], tm + stride, head).wait_send()
-
-    mine = head * width
-
-    def anc_copy(p, to, send, recv):
-        return remote(piece(xa, p, mine), piece(xa, p, mine), send, recv.at[p], tm, to)
-
-    def anc_forward(p):
-        return remote(piece(xa, p, far * width), piece(xa, p, far * width),
-                      anc_send.at[2], anc_f.at[p], tm, sib)
-
-    steps = pieces + 7 * LAG
-
-    def step(s):
-        flow(s, zpos, LINE, 0, x_ref, is_src, zup, szup, up_recv)
-        flow(s, LINE - 1 - zpos, -LINE, 1, x_ref, is_src, zdn, szdn, dn_recv)
-        p = s - 3 * LAG
-        if 0 <= p < pieces:
-            piece(base, p)[...] = jnp.where(
-                is_src, piece(x_ref, p)[...],
-                jnp.where(az < zpos, piece(zup, p)[...], piece(zdn, p)[...]))
-        flow(p, xpos, 1, 2, base, ax == xpos, xr, sxr, xr_recv)
-        flow(p, LINE - 1 - xpos, -1, 3, base, ax == xpos, xl, sxl, xl_recv)
-        p = s - 6 * LAG
-        if 0 <= p < pieces:
-            piece(xa, p, mine)[...] = jnp.where(
-                ax == xpos, piece(base, p)[...],
-                jnp.where(ax < xpos, piece(xr, p)[...], piece(xl, p)[...]))
-            anc_copy(p, far, anc_send.at[0], anc_y).start()
-            anc_copy(p, sib, anc_send.at[1], anc_c).start()
-        p = s - 7 * LAG
-        if 0 <= p < pieces:
-            anc_copy(p, far, anc_send.at[0], anc_y).wait_recv()
-            anc_forward(p).start()
-
-    def norm_project(src, t, first):
-        v = src[:, half(t)].astype(F32)
+    def part(u):
+        return pl.ds(u * rows, rows)
+
+    def quarter(j):
+        return pl.ds(pl.multiple_of(j * COLS, COLS), COLS)
+
+    def row_copy(u, k):
+        return remote(x_ref.at[part(u), quarter(lax.rem(xpos + k, LINE))], got_x.at[k - 1, part(u), :],
+                      row_send.at[u, k - 1], row_recv.at[u, k - 1], in_row(k), head)
+
+    def column_copy(u, k):
+        return remote(here_x.at[part(u), :], got_z.at[k - 1, part(u), :],
+                      col_send.at[u, k - 1], col_recv.at[u, k - 1], in_column(k), head)
+
+    def block(k, u, j):
+        return xa.at[k, pl.ds(pl.multiple_of(j * width + u * rows, 16), rows), :]
+
+    def all_copy(u, k):
+        return remote(block(0, u, head), block(k, u, head),
+                      all_send.at[u, k - 1], all_recv.at[u, k - 1], in_row(k), head)
+
+    def anc_copy(u, k, to, n, recv):
+        return remote(block(k, u, head), block(k, u, head), anc_send.at[n, u, k], recv.at[u, k], tm, to)
+
+    def anc_forward(u, k):
+        return remote(block(k, u, far), block(k, u, far), anc_send.at[2, u, k], anc_f.at[u, k], tm, sib)
+
+    others = (2, 1, 3)
+
+    def row_start():
+        for u in range(PARTS):
+            for k in others:
+                row_copy(u, k).start()
+
+    def pick(which, own, got, u):
+        for k in range(1, LINE):
+            own = jnp.where(which == k, got[k - 1, part(u), :], own)
+        return own
+
+    def row_pick(u):
+        for k in others:
+            row_copy(u, k).wait_recv()
+        here_x[part(u), :] = pick(from_x, x_ref[part(u), quarter(xpos)], got_x, u)
+        for k in others:
+            column_copy(u, k).start()
+
+    def share(u, k):
+        anc_copy(u, k, far, 0, anc_y).start()
+        anc_copy(u, k, sib, 1, anc_c).start()
+
+    def column_pick(u):
+        for k in others:
+            column_copy(u, k).wait_recv()
+        block(0, u, head)[...] = pick(from_z, here_x[part(u), :], got_z, u)
+        for k in others:
+            all_copy(u, k).start()
+        share(u, 0)
+
+    def all_pass(u, k):
+        all_copy(u, k).wait_recv()
+        share(u, k)
+
+    def anc_pass(u, k):
+        anc_copy(u, k, far, 0, anc_y).wait_recv()
+        anc_forward(u, k).start()
+
+    def norm_project(v, first):
+        v = v.astype(F32)
         v = v - jnp.mean(v, axis=0, keepdims=True)
         r = lax.rsqrt(jnp.mean(v * v, axis=0, keepdims=True) + EPSILON)
         n = (v * r * (1.0 + modt[:, 1:2]) + modt[:, 0:1]).astype(BF16)
@@ -180,7 +186,7 @@
     def own_qkv(t):
         for wait in (own_copy(t, sib, own_send.at[1, t], own_c.at[t]), own_forward(t)):
             wait.wait_recv()
-        qkv = norm_project(xf, t, 0)
+        qkv = norm_project(xf[:, half(t)], 0)
         zeros = jnp.zeros((PAD - HS, HALF), F32)
         for h in range(heads):
             q = qkv[h * HS:(h + 1) * HS]
@@ -270,11 +276,7 @@
         ).astype(BF16)
 
     own_start()
-    work = {}
-
-    def after(s, fn, *args):
-        work.setdefault(s, []).append((fn, args))
-
+    row_start()
     def setup():
         modt[...] = mod_ref[...].T
         tapst[...] = taps_ref[...].T
@@ -288,27 +290,51 @@
         def _():
             hr[...] = jnp.zeros_like(hr)
 
+    order = (0, 1, 3, 2)
+    per_half = HALF // COLS
+
     def anchor_kv(t):
-        for p in range(t * HALF // COLS * per_col, (t + 1) * HALF // COLS * per_col):
-            anc_copy(p, sib, anc_send.at[1], anc_c).wait_recv()
-            anc_forward(p).wait_recv()
-        put_kv(norm_project(xa, t, width), t, tokens)
+        ks_of = order[t * per_half:(t + 1) * per_half]
+        for k in ks_of:
+            for u in range(PARTS):
+                anc_copy(u, k, sib, 1, anc_c).wait_recv()
+                anc_forward(u, k).wait_recv()
+        v = jnp.concatenate([xa[k] for k in ks_of], axis=1)
+        put_kv(norm_project(v, width), t, tokens)
 
     units = [(h, t) for t in range(halves) for h in range(heads)]
-    after(1, setup)
-    after(3, own_pass, 0)
-    after(5, own_pass, 1)
-    after(5, own_qkv, 0)
-    after(7, own_qkv, 1)
-    for i, (h, t) in enumerate(units):
-        after(8 + i, attend, h, t, 0, tokens, True, False)
-    after(18, anchor_kv, 0)
-    for i, (h, t) in enumerate(units):
-        after(18 + i // 4, attend, h, t, tokens, HALF, False, False)
-    for s in range(steps):
-        step(s)
-        for fn, args in work.get(s, ()):
-            fn(*args)
+
+    def own_units(lo, hi):
+        for h, t in units[lo:hi]:
+            attend(h, t, 0, tokens, True, False)
+
+    setup()
+    row_pick(0)
+    own_pass(0)
+    row_pick(1)
+    own_qkv(0)
+    own_pass(1)
+    own_qkv(1)
+    own_units(0, 4)
+    column_pick(0)
+    own_units(4, 8)
+    column_pick(1)
+    anc_pass(0, 0)
+    for k in order[1:]:
+        all_pass(0, k)
+    anc_pass(1, 0)
+    all_pass(1, 1)
+    anc_pass(0, 1)
+    all_pass(1, 3)
+    anc_pass(0, 3)
+    all_pass(1, 2)
+    anc_pass(0, 2)
+    anc_pass(1, 1)
+    anc_pass(1, 3)
+    anc_pass(1, 2)
+    anchor_kv(0)
+    for h, t in units:
+        attend(h, t, tokens, HALF, False, False)
 
     def last(h, t):
         attend(h, t, tokens + HALF, HALF, False, True)
@@ -328,13 +354,15 @@
     for t in range(halves):
         finish(t)
 
-    flow_end(zpos, LINE, 0, szup, up_recv)
-    flow_end(LINE - 1 - zpos, -LINE, 1, szdn, dn_recv)
-    flow_end(xpos, 1, 2, sxr, xr_recv)
-    flow_end(LINE - 1 - xpos, -1, 3, sxl, xl_recv)
-    shard = rows_of(xa, head, pl.ds(0, tokens))
-    for n, to in ((0, far), (1, sib), (2, sib)):
-        remote(shard, shard, anc_send.at[n], anc_y.at[0], tm, to).wait_send()
+    for u in range(PARTS):
+        for k in others:
+            row_copy(u, k).wait_send()
+            column_copy(u, k).wait_send()
+            all_copy(u, k).wait_send()
+        for k in range(LINE):
+            anc_copy(u, k, far, 0, anc_y).wait_send()
+            anc_copy(u, k, sib, 1, anc_c).wait_send()
+            anc_forward(u, k).wait_send()
     for t in range(halves):
         own_copy(t, far, own_send.at[0, t], own_y.at[t]).wait_send()
         own_copy(t, sib, own_send.at[1, t], own_c.at[t]).wait_send()
@@ -357,7 +385,6 @@
     d = w_qkv.shape[1]
     heads = width // HS
     halves = tokens // HALF
-    pieces = (width // ROWS) * (tokens // COLS)
     x_t = jnp.swapaxes(frames[0], 0, 1)
     w_t = jnp.swapaxes(w_qkv, 1, 2).reshape(3 * width, d)
     shard = pltpu.VMEM((width, tokens), BF16)
@@ -369,8 +396,9 @@
         in_specs=[vmem] * 5 + [pl.BlockSpec(memory_space=pltpu.SMEM)],
         out_specs=vmem,
         scratch_shapes=[
-            pltpu.VMEM((d, tokens), BF16), pltpu.VMEM((d, tokens), BF16),
-            *[shard] * 9,
+            pltpu.VMEM((d, tokens), BF16), pltpu.VMEM((LINE, d, COLS), BF16),
+            pltpu.VMEM((LINE - 1, width, COLS), BF16), pltpu.VMEM((width, COLS), BF16),
+            pltpu.VMEM((LINE - 1, width, COLS), BF16),
             pltpu.VMEM((d, 3), F32), pltpu.VMEM((width, 3), F32), pltpu.VMEM((d, width), BF16),
             pltpu.VMEM((heads, PAD, tokens), BF16),
             pltpu.VMEM((heads, 2 * tokens, PAD), BF16),
@@ -382,8 +410,8 @@
             pltpu.VMEM((2, width, tokens), F32),
             *[shard] * 5,
             dma((3, halves)), dma((halves,)), dma((halves,)), dma((halves,)),
-            dma((4,)), dma((pieces,)), dma((pieces,)), dma((pieces,)), dma((pieces,)),
-            dma((3,)), dma((pieces,)), dma((pieces,)), dma((pieces,)),
+            *[dma((PARTS, LINE - 1))] * 6,
+            dma((3, PARTS, LINE)), *[dma((PARTS, LINE))] * 3,
             dma((3, halves)), dma((2, halves)), dma((halves,)),
             dma((2, halves)), dma((halves,)), dma((halves,)),
         ],

time: 64.1 us -> 59.7 us (0.931)
  Pallas kernels: 62.3 us -> 57.9 us
    pallas_call x1, Pallas kernels: 62.3 us -> 57.9 us  [local(): pl.pallas_call(kernel, out_shape=jax.ShapeDtypeStruct((width, tokens), BF...]
where the time goes in v3:
time: 59.7 us; the launch traced here: 59.6 us
  Pallas kernels  57.9 us (97%)
  local copies, waits for them, and re-layouts  1.69 us (3%)
    pallas_call x1, Pallas kernels, local(): pl.pallas_call(kernel, out_shape=jax.ShapeDtypeStruct((width, tokens), BF...  57.9 us
    unnamed x1, local copies, waits for them, and re-layouts  1.69 us

profile of v3, /device:TPU:24, one launch (start us, length us, event | category | flops | bytes accessed | tf_op | source)
XLA Modules:
  0.0 59.6 jit_solution(2996836886338644239)
XLA Ops:
  0.0 57.9 %block.1 = bf16[288,512]{1,0:T(8,128)(2,1)} custom-call(bf16[288,512]{1,0:T(8,128)(2,1)} %bitcast.11, f32[3,1152]{1,0:T(4,128)} %mod_ref.1, bf16[864,1152]{1,0:T(8,128)(2,1)} %bitcast.9, bf16[288,1152]{1,0:T(8,128)(2,1)} %wo_ref.1, f32[3,288]{1,0:T(4,128)} %taps_ref.1, s32[4]{0:T(128)} %anchors_ref.1), custom_call_target="tpu_custom_call" | custom-call | tf_op jit(solution)/shard_map/block/pallas_call | solution.py:393
  57.9 1.7 %copy.8 = bf16[1,512,288]{1,2,0:T(8,128)(2,1)} copy(bf16[1,512,288]{1,2,0:T(8,128)(2,1)} %bitcast.10) | data formatting | bytes 589824
